TPU v7x, 32 devices: a whole 2x2x4 slice. The times are simulated.
32 devices in a mesh: dom: 32 (over z, y, x, core).
Axes of the slice: x: 2, y: 2, z: 4, core: 2. Of those that a mesh axis runs over, the one named last changes fastest.
Arguments:
- grad_out: bfloat16 [16384, 256], P('dom'), may hold values from -6 to 6
- states: bfloat16 [16384, 256], P('dom'), may hold values from -0.98828125 to 0.98828125
- slopes: bfloat16 [16384, 256], P('dom'), may hold values from 0.099609375 to 1
- weight: bfloat16 [256, 256], replicated, may hold values from -0.375 to 0.375
- tiles: bfloat16 [768, 128, 128], P('dom'), may hold values from -0.23925781 to 0.23925781
- tile_dst: int32 [768], P('dom'), may hold values from 0 to 3, as said below
- tile_src: int32 [768], P('dom'), may hold values from 0 to 7, as said below
- tile_count: int32 [32], P('dom'), may hold values from 12 to 24, as said below
- send_rows: int32 [128, 128], P('dom'), may hold values from 0 to 511, as said below
Outputs:
- adjoint: float32 [16384, 256], P('dom')
- weight_grad: float32 [256, 256], replicated
Inputs may be any that keep to these rules, and one draw needn't show every extreme that they name: `tile_src`: slot s of a partition with s < 4 has source tile 4 + s; slots 4 to 7 have destination and source tile s - 4; other used slots name a destination below 4 and a source below 8. `tile_dst`: destination tiles of a partition's slots. `tile_count`: some partition uses all 24 slots. `send_rows`: each list holds distinct local rows.
All inputs are finite; a program needn't handle non-finite values.
Results may differ from a plain program's by a relative error of at most 0.009.
Values may be sent and summed in bfloat16 or wider, within the bound.
No kernel may reach another device: no remote copies, remote signals or barrier semaphores. Data moves between devices by JAX's collectives and lax.ppermute only.
A program may use at most 64 MiB of HBM per device.

v0:
```python
import jax
import jax.numpy as jnp
from jax import lax
from jax.sharding import PartitionSpec as P

ITERS = 4
neighbour_steps = (1, -1, 16, -16)


def passed_along(value, axis, steps):
    count = lax.axis_size(axis)
    pairs = [(source, (source + steps) % count) for source in range(count)]
    return lax.ppermute(value, axis, pairs)


def add_tiles(tiles, tile_dst, tile_src, count, extended, total, keep):
    size = tiles.shape[1]
    width = extended.shape[1]
    sources = extended.shape[0] // size
    blocks = total.shape[0] // size
    slots = tiles.shape[0]
    stacked = extended.reshape(sources, size, width)
    index = jnp.minimum(tile_src, sources - 1)
    rows = jnp.take(stacked, index, axis=0)
    prod = jnp.einsum("tij,tjh->tih", tiles, rows, preferred_element_type=jnp.float32)
    used = (jnp.arange(slots, dtype=jnp.int32) < count) & keep(tile_src)
    onehot = (
        (tile_dst[None, :] == jnp.arange(blocks, dtype=jnp.int32)[:, None]) & used[None, :]
    ).astype(jnp.float32)
    summed = jnp.dot(onehot, prod.reshape(slots, size * width), precision=lax.Precision.HIGHEST)
    return summed.reshape(blocks * size, width)


def with_boundary(scaled, send_rows):
    pieces = [scaled]
    for direction in range(4):
        chosen = jnp.take(scaled, send_rows[direction], axis=0)
        pieces.append(passed_along(chosen, "dom", neighbour_steps[direction]))
    return jnp.concatenate(pieces, axis=0)


def propagate(scaled, tiles, tile_dst, tile_src, count, send_rows):
    empty = jnp.zeros(scaled.shape, jnp.float32)
    extended = with_boundary(scaled, send_rows)
    return add_tiles(tiles, tile_dst, tile_src, count, extended, empty, lambda s: s >= 0)


def per_device(grad_out, states, slopes, weight, tiles, tile_dst, tile_src, tile_count, send_rows):
    count = tile_count[0]
    slope_values = slopes.astype(jnp.float32)
    base = grad_out.astype(jnp.float32)
    adjoint = base
    for step in range(ITERS):
        scaled = (slope_values * adjoint).astype(jnp.bfloat16)
        mixed = propagate(scaled, tiles, tile_dst, tile_src, count, send_rows).astype(jnp.bfloat16)
        adjoint = base + lax.dot_general(
            mixed, weight, (((1,), (1,)), ((), ())), preferred_element_type=jnp.float32
        )
    final_scaled = (slope_values * adjoint).astype(jnp.bfloat16)
    node_total = lax.axis_size("dom") * grad_out.shape[0]
    factor = 1.0 / jnp.sqrt(jnp.float32(node_total))
    state_values = states.astype(jnp.float32)
    final_mixed = propagate(final_scaled, tiles, tile_dst, tile_src, count, send_rows)
    grad = lax.psum(
        lax.dot_general(
            state_values, final_mixed, (((0,), (0,)), ((), ())), precision=lax.Precision.HIGHEST
        )
        * factor,
        "dom",
    )
    return (adjoint, grad)


def solution(mesh):
    in_specs = (
        P("dom", None),
        P("dom", None),
        P("dom", None),
        P(),
        P("dom", None, None),
        P("dom"),
        P("dom"),
        P("dom"),
        P("dom", None),
    )
    out_specs = (P("dom", None), P())
    return jax.shard_map(
        per_device, mesh=mesh, in_specs=in_specs, out_specs=out_specs, check_vma=False
    )
```

profile of v0, /device:TPU:0, one launch (start us, length us, event | category | flops | bytes accessed | tf_op | source)
XLA Modules:
  0.0 283.6 jit_solution(12685391604185503891)
XLA Ops:
  10.1 6.5 %collective-permute-start.1 = (bf16[128,256]{1,0:T(8,128)(2,1)S(1)}, bf16[128,256]{1,0:T(8,128)(2,1)S(1)}, u32[]{:S(2)}, u32[]{:S(2)}) collective-permute-start(bf16[128,256]{1,0:T(8,128)(2,1)S(1)} %broadcast_select_fusion.14), channel_id=1, source_target_pairs={{0,31},{1,0},{2,1},{3,2},{4,3},{5,4},{6,5},{7,6},{8,7},{9,8},{10,9... | collective-permute-start | bytes 196616 | tf_op jit(solution)/shard_map/ppermute | solution.py:13
  19.6 3.0 %collective-permute-start.3 = (bf16[128,256]{1,0:T(8,128)(2,1)S(1)}, bf16[128,256]{1,0:T(8,128)(2,1)S(1)}, u32[]{:S(2)}, u32[]{:S(2)}) collective-permute-start(bf16[128,256]{1,0:T(8,128)(2,1)S(1)} %broadcast_select_fusion.4), channel_id=1, source_target_pairs={{0,16},{1,17},{2,18},{3,19},{4,20},{5,21},{6,22},{7,23},{8,24},{9,... | collective-permute-start | bytes 196616 | tf_op jit(solution)/shard_map/ppermute | solution.py:13
  26.6 2.3 convolution_bitcast_fusion.4
  28.9 3.6 %copy.28 = f32[3,8,128,256]{3,1,2,0:T(8,128)} copy(f32[3,8,128,256]{2,3,1,0:T(8,128)} %bitcast.77) | data formatting | bytes 6291456
  32.5 3.1 %convolution_convert_fusion.3 = bf16[4,32768]{1,0:T(4,128)(2,1)S(1)} fusion(pred[4,24]{1,0:T(4,128)(4,1)S(1)} %fusion.24, f32[24,32768]{1,0:T(8,128)} %bitcast.71), kind=kOutput, calls=%fused_computation.28 | convolution fusion | flops 37879808 | bytes 3407968 | tf_op jit(solution)/shard_map/dot_general | solution.py:30
  39.9 5.4 %collective-permute-start.5 = (bf16[128,256]{1,0:T(8,128)(2,1)S(1)}, bf16[128,256]{1,0:T(8,128)(2,1)S(1)}, u32[]{:S(2)}, u32[]{:S(2)}) collective-permute-start(bf16[128,256]{1,0:T(8,128)(2,1)S(1)} %broadcast_select_fusion.13), channel_id=1, source_target_pairs={{0,31},{1,0},{2,1},{3,2},{4,3},{5,4},{6,5},{7,6},{8,7},{9,8},{10,9... | collective-permute-start | bytes 196616 | tf_op jit(solution)/shard_map/ppermute | solution.py:13
  45.4 2.9 %collective-permute-start.7 = (bf16[128,256]{1,0:T(8,128)(2,1)S(1)}, bf16[128,256]{1,0:T(8,128)(2,1)S(1)}, u32[]{:S(2)}, u32[]{:S(2)}) collective-permute-start(bf16[128,256]{1,0:T(8,128)(2,1)S(1)} %broadcast_select_fusion.3), channel_id=1, source_target_pairs={{0,16},{1,17},{2,18},{3,19},{4,20},{5,21},{6,22},{7,23},{8,24},{9,... | collective-permute-start | bytes 196616 | tf_op jit(solution)/shard_map/ppermute | solution.py:13
  48.3 2.8 collective-permute-done.6
  51.8 1.9 gather_fusion.9
  53.6 3.7 %convolution_bitcast_fusion.3 = f32[24,128,256]{1,2,0:T(8,128)} fusion(bf16[24,128,128]{2,1,0:T(8,128)(2,1)S(1)} %copy-done, bf16[24,128,256]{2,1,0:T(8,128)(2,1)} %gather_fusion.9, pred[24]{0:T(512)(128)(4,1)S(1)} %get-tuple-element.10), kind=kOutput, calls=%fused_computation.32 | convolution fusion | flops 202113024 | bytes 5505048 | tf_op jit(solution)/shard_map/tij,tjh->tih/dot_general | solution.py:25
  57.4 3.6 %copy.29 = f32[3,8,128,256]{3,1,2,0:T(8,128)} copy(f32[3,8,128,256]{2,3,1,0:T(8,128)} %bitcast.78) | data formatting | bytes 6291456
  60.9 3.1 %convolution_convert_fusion.2 = bf16[4,32768]{1,0:T(4,128)(2,1)S(1)} fusion(pred[4,24]{1,0:T(4,128)(4,1)S(1)} %fusion.24, f32[24,32768]{1,0:T(8,128)} %bitcast.72), kind=kOutput, calls=%fused_computation.27 | convolution fusion | flops 37879808 | bytes 3407968 | tf_op jit(solution)/shard_map/dot_general | solution.py:30
  68.3 5.6 %collective-permute-start.9 = (bf16[128,256]{1,0:T(8,128)(2,1)S(1)}, bf16[128,256]{1,0:T(8,128)(2,1)S(1)}, u32[]{:S(2)}, u32[]{:S(2)}) collective-permute-start(bf16[128,256]{1,0:T(8,128)(2,1)S(1)} %broadcast_select_fusion.12), channel_id=1, source_target_pairs={{0,31},{1,0},{2,1},{3,2},{4,3},{5,4},{6,5},{7,6},{8,7},{9,8},{10,9... | collective-permute-start | bytes 196616 | tf_op jit(solution)/shard_map/ppermute | solution.py:13
  73.9 2.9 %collective-permute-start.11 = (bf16[128,256]{1,0:T(8,128)(2,1)S(1)}, bf16[128,256]{1,0:T(8,128)(2,1)S(1)}, u32[]{:S(2)}, u32[]{:S(2)}) collective-permute-start(bf16[128,256]{1,0:T(8,128)(2,1)S(1)} %broadcast_select_fusion.2), channel_id=1, source_target_pairs={{0,16},{1,17},{2,18},{3,19},{4,20},{5,21},{6,22},{7,23},{8,24},{9,... | collective-permute-start | bytes 196616 | tf_op jit(solution)/shard_map/ppermute | solution.py:13
  76.8 2.2 collective-permute-done.10
  79.7 1.9 gather_fusion.14
  81.6 3.7 %convolution_bitcast_fusion.2 = f32[24,128,256]{1,2,0:T(8,128)} fusion(bf16[24,128,128]{2,1,0:T(8,128)(2,1)S(1)} %copy-done, bf16[24,128,256]{2,1,0:T(8,128)(2,1)} %gather_fusion.14, pred[24]{0:T(512)(128)(4,1)S(1)} %get-tuple-element.10), kind=kOutput, calls=%fused_computation.31 | convolution fusion | flops 202113024 | bytes 5505048 | tf_op jit(solution)/shard_map/tij,tjh->tih/dot_general | solution.py:25
  85.3 3.6 %copy.30 = f32[3,8,128,256]{3,1,2,0:T(8,128)} copy(f32[3,8,128,256]{2,3,1,0:T(8,128)} %bitcast.79) | data formatting | bytes 6291456
  88.9 3.1 %convolution_convert_fusion.1 = bf16[4,32768]{1,0:T(4,128)(2,1)S(1)} fusion(pred[4,24]{1,0:T(4,128)(4,1)S(1)} %fusion.24, f32[24,32768]{1,0:T(8,128)} %bitcast.73), kind=kOutput, calls=%fused_computation.26 | convolution fusion | flops 37879808 | bytes 3407968 | tf_op jit(solution)/shard_map/dot_general | solution.py:30
  96.2 5.4 %collective-permute-start.13 = (bf16[128,256]{1,0:T(8,128)(2,1)S(1)}, bf16[128,256]{1,0:T(8,128)(2,1)S(1)}, u32[]{:S(2)}, u32[]{:S(2)}) collective-permute-start(bf16[128,256]{1,0:T(8,128)(2,1)S(1)} %broadcast_select_fusion.11), channel_id=1, source_target_pairs={{0,31},{1,0},{2,1},{3,2},{4,3},{5,4},{6,5},{7,6},{8,7},{9,8},{10,9... | collective-permute-start | bytes 196616 | tf_op jit(solution)/shard_map/ppermute | solution.py:13
  102.1 2.5 collective-permute-start.15
  104.6 2.2 collective-permute-done.14
  109.4 3.7 %convolution_bitcast_fusion.1 = f32[24,128,256]{1,2,0:T(8,128)} fusion(bf16[24,128,128]{2,1,0:T(8,128)(2,1)S(1)} %copy-done, bf16[24,128,256]{2,1,0:T(8,128)(2,1)} %gather_fusion.19, pred[24]{0:T(512)(128)(4,1)S(1)} %get-tuple-element.10), kind=kOutput, calls=%fused_computation.30 | convolution fusion | flops 202113024 | bytes 5505048 | tf_op jit(solution)/shard_map/tij,tjh->tih/dot_general | solution.py:25
  113.1 3.6 %copy.31 = f32[3,8,128,256]{3,1,2,0:T(8,128)} copy(f32[3,8,128,256]{2,3,1,0:T(8,128)} %bitcast.80) | data formatting | bytes 6291456
  116.7 3.1 %convolution_convert_fusion = bf16[4,32768]{1,0:T(4,128)(2,1)S(1)} fusion(pred[4,24]{1,0:T(4,128)(4,1)S(1)} %fusion.24, f32[24,32768]{1,0:T(8,128)} %bitcast.74), kind=kOutput, calls=%fused_computation.25 | convolution fusion | flops 37879808 | bytes 3407968 | tf_op jit(solution)/shard_map/dot_general | solution.py:30
  124.8 5.6 %collective-permute-start.17 = (bf16[128,256]{1,0:T(8,128)(2,1)S(1)}, bf16[128,256]{1,0:T(8,128)(2,1)S(1)}, u32[]{:S(2)}, u32[]{:S(2)}) collective-permute-start(bf16[128,256]{1,0:T(8,128)(2,1)S(1)} %broadcast_select_fusion.10), channel_id=1, source_target_pairs={{0,31},{1,0},{2,1},{3,2},{4,3},{5,4},{6,5},{7,6},{8,7},{9,8},{10,9... | collective-permute-start | bytes 196616 | tf_op jit(solution)/shard_map/ppermute | solution.py:13
  130.8 2.5 collective-permute-start.19
  133.4 2.2 collective-permute-done.18
  138.1 3.7 %convolution_bitcast_fusion = f32[24,128,256]{1,2,0:T(8,128)} fusion(bf16[24,128,128]{2,1,0:T(8,128)(2,1)S(1)} %copy-done, bf16[24,128,256]{2,1,0:T(8,128)(2,1)} %gather_fusion.24, pred[24]{0:T(512)(128)(4,1)S(1)} %get-tuple-element.10), kind=kOutput, calls=%fused_computation.29 | convolution fusion | flops 202113024 | bytes 5505048 | tf_op jit(solution)/shard_map/tij,tjh->tih/dot_general | solution.py:25
  141.9 3.6 %copy.32 = f32[3,8,128,256]{3,1,2,0:T(8,128)} copy(f32[3,8,128,256]{2,3,1,0:T(8,128)} %bitcast.75) | data formatting | bytes 6291456
  145.4 3.1 %fusion.32 = f32[4,32768]{1,0:T(4,128)S(1)} fusion(pred[4,24]{1,0:T(4,128)(4,1)S(1)} %fusion.24, f32[24,32768]{1,0:T(8,128)} %bitcast.76), kind=kOutput, calls=%fused_computation.133 | convolution fusion | flops 37748736 | bytes 3670112 | tf_op jit(solution)/shard_map/dot_general | solution.py:30
  150.2 124.7 %all-reduce.2.cloned.1.call-done = f32[256,256]{0,1:T(8,128)} async-done(((f32[256,256]{0,1:T(8,128)}), f32[256,256]{0,1:T(8,128)}) %all-reduce.2.cloned.1.call-update) | async-done | bytes 262160 | tf_op jit(solution)/shard_map/psum | solution.py:64
  (125 shorter events, 37.8 us)
Async XLA Ops:
  7.2 19.4 %copy-start = (bf16[24,128,128]{2,1,0:T(8,128)(2,1)S(1)}, bf16[24,128,128]{2,1,0:T(8,128)(2,1)}, u32[]{:S(2)}) copy-start(bf16[24,128,128]{2,1,0:T(8,128)(2,1)} %param.17) | copy-start | bytes 2359300
  7.2 267.8 %all-reduce.2.cloned.1.call-start = ((), (), s32[]{:S(2)}) async-start(), calls=%async_computation | async-start | bytes 524288 | tf_op jit(solution)/shard_map/psum | solution.py:64
  9.2 14.0 %copy-start.5 = (s32[24]{0:T(128)S(1)}, s32[24]{0:T(128)}, u32[]{:S(2)}) copy-start(s32[24]{0:T(128)} %param.19) | copy-start | bytes 292
  9.2 14.1 %copy-start.6 = (s32[24]{0:T(128)S(1)}, s32[24]{0:T(128)}, u32[]{:S(2)}) copy-start(s32[24]{0:T(128)} %param.18) | copy-start | bytes 292
  10.1 14.8 %collective-permute-start.1 = (bf16[128,256]{1,0:T(8,128)(2,1)S(1)}, bf16[128,256]{1,0:T(8,128)(2,1)S(1)}, u32[]{:S(2)}, u32[]{:S(2)}) collective-permute-start(bf16[128,256]{1,0:T(8,128)(2,1)S(1)} %broadcast_select_fusion.14), channel_id=1, source_target_pairs={{0,31},{1,0},{2,1},{3,2},{4,3},{5,4},{6,5},{7,6},{8,7},{9,8},{10,9... | collective-permute-start | bytes 196616 | tf_op jit(solution)/shard_map/ppermute | solution.py:13
  17.5 7.4 %collective-permute-start = (bf16[128,256]{1,0:T(8,128)(2,1)S(1)}, bf16[128,256]{1,0:T(8,128)(2,1)S(1)}, u32[]{:S(2)}, u32[]{:S(2)}) collective-permute-start(bf16[128,256]{1,0:T(8,128)(2,1)S(1)} %broadcast_select_fusion.19), channel_id=1, source_target_pairs={{0,1},{1,2},{2,3},{3,4},{4,5},{5,6},{6,7},{7,8},{8,9},{9,10},{10,1... | collective-permute-start | bytes 196616 | tf_op jit(solution)/shard_map/ppermute | solution.py:13
  18.6 6.4 %collective-permute-start.2 = (bf16[128,256]{1,0:T(8,128)(2,1)S(1)}, bf16[128,256]{1,0:T(8,128)(2,1)S(1)}, u32[]{:S(2)}, u32[]{:S(2)}) collective-permute-start(bf16[128,256]{1,0:T(8,128)(2,1)S(1)} %broadcast_select_fusion.9), channel_id=1, source_target_pairs={{0,16},{1,17},{2,18},{3,19},{4,20},{5,21},{6,22},{7,23},{8,24},{9,... | collective-permute-start | bytes 196616 | tf_op jit(solution)/shard_map/ppermute | solution.py:13
  19.6 6.3 %collective-permute-start.3 = (bf16[128,256]{1,0:T(8,128)(2,1)S(1)}, bf16[128,256]{1,0:T(8,128)(2,1)S(1)}, u32[]{:S(2)}, u32[]{:S(2)}) collective-permute-start(bf16[128,256]{1,0:T(8,128)(2,1)S(1)} %broadcast_select_fusion.4), channel_id=1, source_target_pairs={{0,16},{1,17},{2,18},{3,19},{4,20},{5,21},{6,22},{7,23},{8,24},{9,... | collective-permute-start | bytes 196616 | tf_op jit(solution)/shard_map/ppermute | solution.py:13
  32.5 3.3 %copy-start.1 = (bf16[512,256]{1,0:T(8,128)(2,1)S(1)}, bf16[512,256]{1,0:T(8,128)(2,1)}, u32[]{:S(2)}) copy-start(bf16[512,256]{1,0:T(8,128)(2,1)} %param.15) | copy-start | bytes 786436
  32.5 3.3 %copy-start.2 = (bf16[512,256]{1,0:T(8,128)(2,1)S(1)}, bf16[512,256]{1,0:T(8,128)(2,1)}, u32[]{:S(2)}) copy-start(bf16[512,256]{1,0:T(8,128)(2,1)} %param.13) | copy-start | bytes 786436
  32.5 3.4 %copy-start.3 = (bf16[256,256]{1,0:T(8,128)(2,1)S(1)}, bf16[256,256]{1,0:T(8,128)(2,1)}, u32[]{:S(2)}) copy-start(bf16[256,256]{1,0:T(8,128)(2,1)} %param.16) | copy-start | bytes 393220
  39.8 8.5 %collective-permute-start.4 = (bf16[128,256]{1,0:T(8,128)(2,1)S(1)}, bf16[128,256]{1,0:T(8,128)(2,1)S(1)}, u32[]{:S(2)}, u32[]{:S(2)}) collective-permute-start(bf16[128,256]{1,0:T(8,128)(2,1)S(1)} %broadcast_select_fusion.18), channel_id=1, source_target_pairs={{0,1},{1,2},{2,3},{3,4},{4,5},{5,6},{6,7},{7,8},{8,9},{9,10},{10,1... | collective-permute-start | bytes 196616 | tf_op jit(solution)/shard_map/ppermute | solution.py:13
  39.9 8.3 %collective-permute-start.5 = (bf16[128,256]{1,0:T(8,128)(2,1)S(1)}, bf16[128,256]{1,0:T(8,128)(2,1)S(1)}, u32[]{:S(2)}, u32[]{:S(2)}) collective-permute-start(bf16[128,256]{1,0:T(8,128)(2,1)S(1)} %broadcast_select_fusion.13), channel_id=1, source_target_pairs={{0,31},{1,0},{2,1},{3,2},{4,3},{5,4},{6,5},{7,6},{8,7},{9,8},{10,9... | collective-permute-start | bytes 196616 | tf_op jit(solution)/shard_map/ppermute | solution.py:13
  45.3 5.7 %collective-permute-start.6 = (bf16[128,256]{1,0:T(8,128)(2,1)S(1)}, bf16[128,256]{1,0:T(8,128)(2,1)S(1)}, u32[]{:S(2)}, u32[]{:S(2)}) collective-permute-start(bf16[128,256]{1,0:T(8,128)(2,1)S(1)} %broadcast_select_fusion.8), channel_id=1, source_target_pairs={{0,16},{1,17},{2,18},{3,19},{4,20},{5,21},{6,22},{7,23},{8,24},{9,... | collective-permute-start | bytes 196616 | tf_op jit(solution)/shard_map/ppermute | solution.py:13
  45.4 6.4 %collective-permute-start.7 = (bf16[128,256]{1,0:T(8,128)(2,1)S(1)}, bf16[128,256]{1,0:T(8,128)(2,1)S(1)}, u32[]{:S(2)}, u32[]{:S(2)}) collective-permute-start(bf16[128,256]{1,0:T(8,128)(2,1)S(1)} %broadcast_select_fusion.3), channel_id=1, source_target_pairs={{0,16},{1,17},{2,18},{3,19},{4,20},{5,21},{6,22},{7,23},{8,24},{9,... | collective-permute-start | bytes 196616 | tf_op jit(solution)/shard_map/ppermute | solution.py:13
  68.1 8.6 %collective-permute-start.8 = (bf16[128,256]{1,0:T(8,128)(2,1)S(1)}, bf16[128,256]{1,0:T(8,128)(2,1)S(1)}, u32[]{:S(2)}, u32[]{:S(2)}) collective-permute-start(bf16[128,256]{1,0:T(8,128)(2,1)S(1)} %broadcast_select_fusion.17), channel_id=1, source_target_pairs={{0,1},{1,2},{2,3},{3,4},{4,5},{5,6},{6,7},{7,8},{8,9},{9,10},{10,1... | collective-permute-start | bytes 196616 | tf_op jit(solution)/shard_map/ppermute | solution.py:13
  68.3 8.5 %collective-permute-start.9 = (bf16[128,256]{1,0:T(8,128)(2,1)S(1)}, bf16[128,256]{1,0:T(8,128)(2,1)S(1)}, u32[]{:S(2)}, u32[]{:S(2)}) collective-permute-start(bf16[128,256]{1,0:T(8,128)(2,1)S(1)} %broadcast_select_fusion.12), channel_id=1, source_target_pairs={{0,31},{1,0},{2,1},{3,2},{4,3},{5,4},{6,5},{7,6},{8,7},{9,8},{10,9... | collective-permute-start | bytes 196616 | tf_op jit(solution)/shard_map/ppermute | solution.py:13
  73.9 5.2 %collective-permute-start.10 = (bf16[128,256]{1,0:T(8,128)(2,1)S(1)}, bf16[128,256]{1,0:T(8,128)(2,1)S(1)}, u32[]{:S(2)}, u32[]{:S(2)}) collective-permute-start(bf16[128,256]{1,0:T(8,128)(2,1)S(1)} %broadcast_select_fusion.7), channel_id=1, source_target_pairs={{0,16},{1,17},{2,18},{3,19},{4,20},{5,21},{6,22},{7,23},{8,24},{9,... | collective-permute-start | bytes 196616 | tf_op jit(solution)/shard_map/ppermute | solution.py:13
  73.9 5.9 %collective-permute-start.11 = (bf16[128,256]{1,0:T(8,128)(2,1)S(1)}, bf16[128,256]{1,0:T(8,128)(2,1)S(1)}, u32[]{:S(2)}, u32[]{:S(2)}) collective-permute-start(bf16[128,256]{1,0:T(8,128)(2,1)S(1)} %broadcast_select_fusion.2), channel_id=1, source_target_pairs={{0,16},{1,17},{2,18},{3,19},{4,20},{5,21},{6,22},{7,23},{8,24},{9,... | collective-permute-start | bytes 196616 | tf_op jit(solution)/shard_map/ppermute | solution.py:13
  96.1 8.5 %collective-permute-start.12 = (bf16[128,256]{1,0:T(8,128)(2,1)S(1)}, bf16[128,256]{1,0:T(8,128)(2,1)S(1)}, u32[]{:S(2)}, u32[]{:S(2)}) collective-permute-start(bf16[128,256]{1,0:T(8,128)(2,1)S(1)} %broadcast_select_fusion.16), channel_id=1, source_target_pairs={{0,1},{1,2},{2,3},{3,4},{4,5},{5,6},{6,7},{7,8},{8,9},{9,10},{10,1... | collective-permute-start | bytes 196616 | tf_op jit(solution)/shard_map/ppermute | solution.py:13
  96.2 8.3 %collective-permute-start.13 = (bf16[128,256]{1,0:T(8,128)(2,1)S(1)}, bf16[128,256]{1,0:T(8,128)(2,1)S(1)}, u32[]{:S(2)}, u32[]{:S(2)}) collective-permute-start(bf16[128,256]{1,0:T(8,128)(2,1)S(1)} %broadcast_select_fusion.11), channel_id=1, source_target_pairs={{0,31},{1,0},{2,1},{3,2},{4,3},{5,4},{6,5},{7,6},{8,7},{9,8},{10,9... | collective-permute-start | bytes 196616 | tf_op jit(solution)/shard_map/ppermute | solution.py:13
  101.6 5.2 %collective-permute-start.14 = (bf16[128,256]{1,0:T(8,128)(2,1)S(1)}, bf16[128,256]{1,0:T(8,128)(2,1)S(1)}, u32[]{:S(2)}, u32[]{:S(2)}) collective-permute-start(bf16[128,256]{1,0:T(8,128)(2,1)S(1)} %broadcast_select_fusion.6), channel_id=1, source_target_pairs={{0,16},{1,17},{2,18},{3,19},{4,20},{5,21},{6,22},{7,23},{8,24},{9,... | collective-permute-start | bytes 196616 | tf_op jit(solution)/shard_map/ppermute | solution.py:13
  102.1 5.4 %collective-permute-start.15 = (bf16[128,256]{1,0:T(8,128)(2,1)S(1)}, bf16[128,256]{1,0:T(8,128)(2,1)S(1)}, u32[]{:S(2)}, u32[]{:S(2)}) collective-permute-start(bf16[128,256]{1,0:T(8,128)(2,1)S(1)} %broadcast_select_fusion.1), channel_id=1, source_target_pairs={{0,16},{1,17},{2,18},{3,19},{4,20},{5,21},{6,22},{7,23},{8,24},{9,... | collective-permute-start | bytes 196616 | tf_op jit(solution)/shard_map/ppermute | solution.py:13
  124.6 8.7 %collective-permute-start.16 = (bf16[128,256]{1,0:T(8,128)(2,1)S(1)}, bf16[128,256]{1,0:T(8,128)(2,1)S(1)}, u32[]{:S(2)}, u32[]{:S(2)}) collective-permute-start(bf16[128,256]{1,0:T(8,128)(2,1)S(1)} %broadcast_select_fusion.15), channel_id=1, source_target_pairs={{0,1},{1,2},{2,3},{3,4},{4,5},{5,6},{6,7},{7,8},{8,9},{9,10},{10,1... | collective-permute-start | bytes 196616 | tf_op jit(solution)/shard_map/ppermute | solution.py:13
  124.8 8.5 %collective-permute-start.17 = (bf16[128,256]{1,0:T(8,128)(2,1)S(1)}, bf16[128,256]{1,0:T(8,128)(2,1)S(1)}, u32[]{:S(2)}, u32[]{:S(2)}) collective-permute-start(bf16[128,256]{1,0:T(8,128)(2,1)S(1)} %broadcast_select_fusion.10), channel_id=1, source_target_pairs={{0,31},{1,0},{2,1},{3,2},{4,3},{5,4},{6,5},{7,6},{8,7},{9,8},{10,9... | collective-permute-start | bytes 196616 | tf_op jit(solution)/shard_map/ppermute | solution.py:13
  130.4 5.2 %collective-permute-start.18 = (bf16[128,256]{1,0:T(8,128)(2,1)S(1)}, bf16[128,256]{1,0:T(8,128)(2,1)S(1)}, u32[]{:S(2)}, u32[]{:S(2)}) collective-permute-start(bf16[128,256]{1,0:T(8,128)(2,1)S(1)} %broadcast_select_fusion.5), channel_id=1, source_target_pairs={{0,16},{1,17},{2,18},{3,19},{4,20},{5,21},{6,22},{7,23},{8,24},{9,... | collective-permute-start | bytes 196616 | tf_op jit(solution)/shard_map/ppermute | solution.py:13
  130.8 5.4 %collective-permute-start.19 = (bf16[128,256]{1,0:T(8,128)(2,1)S(1)}, bf16[128,256]{1,0:T(8,128)(2,1)S(1)}, u32[]{:S(2)}, u32[]{:S(2)}) collective-permute-start(bf16[128,256]{1,0:T(8,128)(2,1)S(1)} %broadcast_select_fusion), channel_id=1, source_target_pairs={{0,16},{1,17},{2,18},{3,19},{4,20},{5,21},{6,22},{7,23},{8,24},{9,... | collective-permute-start | bytes 196616 | tf_op jit(solution)/shard_map/ppermute | solution.py:13
  145.4 3.5 %copy-start.4 = (bf16[512,256]{1,0:T(8,128)(2,1)S(1)}, bf16[512,256]{1,0:T(8,128)(2,1)}, u32[]{:S(2)}) copy-start(bf16[512,256]{1,0:T(8,128)(2,1)} %param.14) | copy-start | bytes 786436
Sparse Core Ops, SparseCore 0:
  150.4 124.5 all-reduce.1
where the time goes:
time: 284 us
  waiting for transfers between devices  139 us (49%)
  local copies, waits for them, and re-layouts  45.8 us (16%)
  starting transfers between devices  43.4 us (15%)
  matrix products  35.9 us (13%)
  between operations  15.2 us (5%)
  other arithmetic  3.69 us (1%)
    psum x1, waiting for transfers between devices, per_device(): lax.psum(lax.dot_general(state_values, final_mixed, (((0,), (0,)), ((), (...  125 us
    ppermute x20, starting transfers between devices, passed_along(): return lax.ppermute(value, axis, pairs)  43.4 us
    unnamed x35, local copies, waits for them, and re-layouts  19.7 us
    dot_general x5, matrix products, add_tiles(): jnp.einsum('tij,tjh->tih', tiles, rows, preferred_element_type=jnp.float32)  17.2 us
    gather x20, local copies, waits for them, and re-layouts, with_boundary(): chosen = jnp.take(scaled, send_rows[direction], axis=0)  16.9 us
    dot_general x5, matrix products, add_tiles(): jnp.dot(onehot, prod.reshape(slots, size * width), precision=lax.Precisio...  15.5 us
    ppermute x20, waiting for transfers between devices, passed_along(): return lax.ppermute(value, axis, pairs)  14.8 us
    gather x5, local copies, waits for them, and re-layouts, add_tiles(): rows = jnp.take(stacked, index, axis=0)  8.06 us
  transfers between devices with their start and end apart: 21, of which 11 were waited for; matrix products, arithmetic and copies ran while one was open for 1% of the time, Pallas kernels for 0%

commit v1 on v0

--- a/solution.py
+++ b/solution.py
@@ -61,12 +61,15 @@
     factor = 1.0 / jnp.sqrt(jnp.float32(node_total))
     state_values = states.astype(jnp.float32)
     final_mixed = propagate(final_scaled, tiles, tile_dst, tile_src, count, send_rows)
-    grad = lax.psum(
-        lax.dot_general(
-            state_values, final_mixed, (((0,), (0,)), ((), ())), precision=lax.Precision.HIGHEST
-        )
-        * factor,
-        "dom",
+    grad = jnp.sum(
+        lax.all_gather(
+            lax.dot_general(
+                state_values, final_mixed, (((0,), (0,)), ((), ())), precision=lax.Precision.HIGHEST
+            )
+            * factor,
+            "dom",
+        ),
+        axis=0,
     )
     return (adjoint, grad)
 

time: 284 us -> 249 us (0.88)
  waiting for transfers between devices: 139 us -> 97 us
  local copies, waits for them, and re-layouts: 45.8 us -> 51.7 us
    psum x1 -> x0, waiting for transfers between devices: 125 us -> none  [per_device(): lax.psum(lax.dot_general(state_values, final_mixed, (((0,), (0,)), ((), (...]
    all_gather x0 -> x1, waiting for transfers between devices: none -> 82.2 us  [per_device(): lax.all_gather(lax.dot_general(state_values, final_mixed, (((0,), (0,)),...]
    unnamed x35 -> x36, local copies, waits for them, and re-layouts: 19.7 us -> 25.6 us
where the time goes in v1:
time: 249 us
  waiting for transfers between devices  97 us (39%)
  local copies, waits for them, and re-layouts  51.7 us (21%)
  starting transfers between devices  43.4 us (17%)
  matrix products  35.9 us (14%)
  between operations  15.3 us (6%)
  other arithmetic  5.62 us (2%)
    all_gather x1, waiting for transfers between devices, per_device(): lax.all_gather(lax.dot_general(state_values, final_mixed, (((0,), (0,)),...  82.2 us
    ppermute x20, starting transfers between devices, passed_along(): return lax.ppermute(value, axis, pairs)  43.4 us
    unnamed x36, local copies, waits for them, and re-layouts  25.6 us
    dot_general x5, matrix products, add_tiles(): jnp.einsum('tij,tjh->tih', tiles, rows, preferred_element_type=jnp.float32)  17.2 us
    gather x20, local copies, waits for them, and re-layouts, with_boundary(): chosen = jnp.take(scaled, send_rows[direction], axis=0)  16.9 us
    dot_general x5, matrix products, add_tiles(): jnp.dot(onehot, prod.reshape(slots, size * width), precision=lax.Precisio...  15.5 us
    ppermute x20, waiting for transfers between devices, passed_along(): return lax.ppermute(value, axis, pairs)  14.8 us
    gather x5, local copies, waits for them, and re-layouts, add_tiles(): rows = jnp.take(stacked, index, axis=0)  8.06 us
  transfers between devices with their start and end apart: 21, of which 11 were waited for; matrix products, arithmetic and copies ran while one was open for 1% of the time, Pallas kernels for 0%

profile of v1, /device:TPU:0, one launch (start us, length us, event | category | flops | bytes accessed | tf_op | source)
XLA Modules:
  0.0 248.9 jit_solution(16563301579250231544)
XLA Ops:
  10.1 6.5 %collective-permute-start.1 = (bf16[128,256]{1,0:T(8,128)(2,1)S(1)}, bf16[128,256]{1,0:T(8,128)(2,1)S(1)}, u32[]{:S(2)}, u32[]{:S(2)}) collective-permute-start(bf16[128,256]{1,0:T(8,128)(2,1)S(1)} %broadcast_select_fusion.14), channel_id=1, source_target_pairs={{0,31},{1,0},{2,1},{3,2},{4,3},{5,4},{6,5},{7,6},{8,7},{9,8},{10,9... | collective-permute-start | bytes 196616 | tf_op jit(solution)/shard_map/ppermute | solution.py:13
  19.6 3.0 %collective-permute-start.3 = (bf16[128,256]{1,0:T(8,128)(2,1)S(1)}, bf16[128,256]{1,0:T(8,128)(2,1)S(1)}, u32[]{:S(2)}, u32[]{:S(2)}) collective-permute-start(bf16[128,256]{1,0:T(8,128)(2,1)S(1)} %broadcast_select_fusion.4), channel_id=1, source_target_pairs={{0,16},{1,17},{2,18},{3,19},{4,20},{5,21},{6,22},{7,23},{8,24},{9,... | collective-permute-start | bytes 196616 | tf_op jit(solution)/shard_map/ppermute | solution.py:13
  26.6 2.3 convolution_bitcast_fusion.4
  28.9 3.6 %copy.37 = f32[3,8,128,256]{3,1,2,0:T(8,128)} copy(f32[3,8,128,256]{2,3,1,0:T(8,128)} %bitcast.82) | data formatting | bytes 6291456
  32.5 3.1 %convolution_convert_fusion.3 = bf16[4,32768]{1,0:T(4,128)(2,1)S(1)} fusion(pred[4,24]{1,0:T(4,128)(4,1)S(1)} %fusion.24, f32[24,32768]{1,0:T(8,128)} %bitcast.76), kind=kOutput, calls=%fused_computation.28 | convolution fusion | flops 37879808 | bytes 3407968 | tf_op jit(solution)/shard_map/dot_general | solution.py:30
  39.9 5.4 %collective-permute-start.5 = (bf16[128,256]{1,0:T(8,128)(2,1)S(1)}, bf16[128,256]{1,0:T(8,128)(2,1)S(1)}, u32[]{:S(2)}, u32[]{:S(2)}) collective-permute-start(bf16[128,256]{1,0:T(8,128)(2,1)S(1)} %broadcast_select_fusion.13), channel_id=1, source_target_pairs={{0,31},{1,0},{2,1},{3,2},{4,3},{5,4},{6,5},{7,6},{8,7},{9,8},{10,9... | collective-permute-start | bytes 196616 | tf_op jit(solution)/shard_map/ppermute | solution.py:13
  45.4 2.9 %collective-permute-start.7 = (bf16[128,256]{1,0:T(8,128)(2,1)S(1)}, bf16[128,256]{1,0:T(8,128)(2,1)S(1)}, u32[]{:S(2)}, u32[]{:S(2)}) collective-permute-start(bf16[128,256]{1,0:T(8,128)(2,1)S(1)} %broadcast_select_fusion.3), channel_id=1, source_target_pairs={{0,16},{1,17},{2,18},{3,19},{4,20},{5,21},{6,22},{7,23},{8,24},{9,... | collective-permute-start | bytes 196616 | tf_op jit(solution)/shard_map/ppermute | solution.py:13
  48.3 2.8 %collective-permute-done.6 = bf16[128,256]{1,0:T(8,128)(2,1)S(1)} collective-permute-done((bf16[128,256]{1,0:T(8,128)(2,1)S(1)}, bf16[128,256]{1,0:T(8,128)(2,1)S(1)}, u32[]{:S(2)}, u32[]{:S(2)}) %collective-permute-start.6) | collective-permute-done | bytes 65568 | tf_op jit(solution)/shard_map/ppermute | solution.py:13
  53.6 3.7 %convolution_bitcast_fusion.3 = f32[24,128,256]{1,2,0:T(8,128)} fusion(bf16[24,128,128]{2,1,0:T(8,128)(2,1)S(1)} %copy-done, bf16[24,128,256]{2,1,0:T(8,128)(2,1)} %gather_fusion.9, pred[24]{0:T(512)(128)(4,1)S(1)} %get-tuple-element.8), kind=kOutput, calls=%fused_computation.33 | convolution fusion | flops 202113024 | bytes 5505048 | tf_op jit(solution)/shard_map/tij,tjh->tih/dot_general | solution.py:25
  57.4 3.6 %copy.38 = f32[3,8,128,256]{3,1,2,0:T(8,128)} copy(f32[3,8,128,256]{2,3,1,0:T(8,128)} %bitcast.83) | data formatting | bytes 6291456
  60.9 3.1 %convolution_convert_fusion.2 = bf16[4,32768]{1,0:T(4,128)(2,1)S(1)} fusion(pred[4,24]{1,0:T(4,128)(4,1)S(1)} %fusion.24, f32[24,32768]{1,0:T(8,128)} %bitcast.77), kind=kOutput, calls=%fused_computation.27 | convolution fusion | flops 37879808 | bytes 3407968 | tf_op jit(solution)/shard_map/dot_general | solution.py:30
  68.3 5.6 %collective-permute-start.9 = (bf16[128,256]{1,0:T(8,128)(2,1)S(1)}, bf16[128,256]{1,0:T(8,128)(2,1)S(1)}, u32[]{:S(2)}, u32[]{:S(2)}) collective-permute-start(bf16[128,256]{1,0:T(8,128)(2,1)S(1)} %broadcast_select_fusion.12), channel_id=1, source_target_pairs={{0,31},{1,0},{2,1},{3,2},{4,3},{5,4},{6,5},{7,6},{8,7},{9,8},{10,9... | collective-permute-start | bytes 196616 | tf_op jit(solution)/shard_map/ppermute | solution.py:13
  73.9 2.9 %collective-permute-start.11 = (bf16[128,256]{1,0:T(8,128)(2,1)S(1)}, bf16[128,256]{1,0:T(8,128)(2,1)S(1)}, u32[]{:S(2)}, u32[]{:S(2)}) collective-permute-start(bf16[128,256]{1,0:T(8,128)(2,1)S(1)} %broadcast_select_fusion.2), channel_id=1, source_target_pairs={{0,16},{1,17},{2,18},{3,19},{4,20},{5,21},{6,22},{7,23},{8,24},{9,... | collective-permute-start | bytes 196616 | tf_op jit(solution)/shard_map/ppermute | solution.py:13
  76.8 2.2 collective-permute-done.10
  81.6 3.7 %convolution_bitcast_fusion.2 = f32[24,128,256]{1,2,0:T(8,128)} fusion(bf16[24,128,128]{2,1,0:T(8,128)(2,1)S(1)} %copy-done, bf16[24,128,256]{2,1,0:T(8,128)(2,1)} %gather_fusion.14, pred[24]{0:T(512)(128)(4,1)S(1)} %get-tuple-element.8), kind=kOutput, calls=%fused_computation.32 | convolution fusion | flops 202113024 | bytes 5505048 | tf_op jit(solution)/shard_map/tij,tjh->tih/dot_general | solution.py:25
  85.3 3.6 %copy.39 = f32[3,8,128,256]{3,1,2,0:T(8,128)} copy(f32[3,8,128,256]{2,3,1,0:T(8,128)} %bitcast.84) | data formatting | bytes 6291456
  88.9 3.1 %convolution_convert_fusion.1 = bf16[4,32768]{1,0:T(4,128)(2,1)S(1)} fusion(pred[4,24]{1,0:T(4,128)(4,1)S(1)} %fusion.24, f32[24,32768]{1,0:T(8,128)} %bitcast.78), kind=kOutput, calls=%fused_computation.26 | convolution fusion | flops 37879808 | bytes 3407968 | tf_op jit(solution)/shard_map/dot_general | solution.py:30
  96.2 5.4 %collective-permute-start.13 = (bf16[128,256]{1,0:T(8,128)(2,1)S(1)}, bf16[128,256]{1,0:T(8,128)(2,1)S(1)}, u32[]{:S(2)}, u32[]{:S(2)}) collective-permute-start(bf16[128,256]{1,0:T(8,128)(2,1)S(1)} %broadcast_select_fusion.11), channel_id=1, source_target_pairs={{0,31},{1,0},{2,1},{3,2},{4,3},{5,4},{6,5},{7,6},{8,7},{9,8},{10,9... | collective-permute-start | bytes 196616 | tf_op jit(solution)/shard_map/ppermute | solution.py:13
  102.1 2.5 %collective-permute-start.15 = (bf16[128,256]{1,0:T(8,128)(2,1)S(1)}, bf16[128,256]{1,0:T(8,128)(2,1)S(1)}, u32[]{:S(2)}, u32[]{:S(2)}) collective-permute-start(bf16[128,256]{1,0:T(8,128)(2,1)S(1)} %broadcast_select_fusion.1), channel_id=1, source_target_pairs={{0,16},{1,17},{2,18},{3,19},{4,20},{5,21},{6,22},{7,23},{8,24},{9,... | collective-permute-start | bytes 196616 | tf_op jit(solution)/shard_map/ppermute | solution.py:13
  104.6 2.2 collective-permute-done.14
  109.4 3.7 %convolution_bitcast_fusion.1 = f32[24,128,256]{1,2,0:T(8,128)} fusion(bf16[24,128,128]{2,1,0:T(8,128)(2,1)S(1)} %copy-done, bf16[24,128,256]{2,1,0:T(8,128)(2,1)} %gather_fusion.19, pred[24]{0:T(512)(128)(4,1)S(1)} %get-tuple-element.8), kind=kOutput, calls=%fused_computation.31 | convolution fusion | flops 202113024 | bytes 5505048 | tf_op jit(solution)/shard_map/tij,tjh->tih/dot_general | solution.py:25
  113.1 3.6 %copy.40 = f32[3,8,128,256]{3,1,2,0:T(8,128)} copy(f32[3,8,128,256]{2,3,1,0:T(8,128)} %bitcast.85) | data formatting | bytes 6291456
  116.7 3.1 %convolution_convert_fusion = bf16[4,32768]{1,0:T(4,128)(2,1)S(1)} fusion(pred[4,24]{1,0:T(4,128)(4,1)S(1)} %fusion.24, f32[24,32768]{1,0:T(8,128)} %bitcast.79), kind=kOutput, calls=%fused_computation.25 | convolution fusion | flops 37879808 | bytes 3407968 | tf_op jit(solution)/shard_map/dot_general | solution.py:30
  124.8 5.6 %collective-permute-start.17 = (bf16[128,256]{1,0:T(8,128)(2,1)S(1)}, bf16[128,256]{1,0:T(8,128)(2,1)S(1)}, u32[]{:S(2)}, u32[]{:S(2)}) collective-permute-start(bf16[128,256]{1,0:T(8,128)(2,1)S(1)} %broadcast_select_fusion.10), channel_id=1, source_target_pairs={{0,31},{1,0},{2,1},{3,2},{4,3},{5,4},{6,5},{7,6},{8,7},{9,8},{10,9... | collective-permute-start | bytes 196616 | tf_op jit(solution)/shard_map/ppermute | solution.py:13
  130.8 2.5 %collective-permute-start.19 = (bf16[128,256]{1,0:T(8,128)(2,1)S(1)}, bf16[128,256]{1,0:T(8,128)(2,1)S(1)}, u32[]{:S(2)}, u32[]{:S(2)}) collective-permute-start(bf16[128,256]{1,0:T(8,128)(2,1)S(1)} %broadcast_select_fusion), channel_id=1, source_target_pairs={{0,16},{1,17},{2,18},{3,19},{4,20},{5,21},{6,22},{7,23},{8,24},{9,... | collective-permute-start | bytes 196616 | tf_op jit(solution)/shard_map/ppermute | solution.py:13
  133.4 2.2 collective-permute-done.18
  138.1 3.7 %convolution_bitcast_fusion = f32[24,128,256]{1,2,0:T(8,128)} fusion(bf16[24,128,128]{2,1,0:T(8,128)(2,1)S(1)} %copy-done, bf16[24,128,256]{2,1,0:T(8,128)(2,1)} %gather_fusion.24, pred[24]{0:T(512)(128)(4,1)S(1)} %get-tuple-element.8), kind=kOutput, calls=%fused_computation.30 | convolution fusion | flops 202113024 | bytes 5505048 | tf_op jit(solution)/shard_map/tij,tjh->tih/dot_general | solution.py:25
  141.9 3.6 %copy.41 = f32[3,8,128,256]{3,1,2,0:T(8,128)} copy(f32[3,8,128,256]{2,3,1,0:T(8,128)} %bitcast.80) | data formatting | bytes 6291456
  145.4 3.1 %fusion.32 = f32[4,32768]{1,0:T(4,128)S(1)} fusion(pred[4,24]{1,0:T(4,128)(4,1)S(1)} %fusion.24, f32[24,32768]{1,0:T(8,128)} %bitcast.81), kind=kOutput, calls=%fused_computation.134 | convolution fusion | flops 37748736 | bytes 3670112 | tf_op jit(solution)/shard_map/dot_general | solution.py:30
  150.2 82.2 %all-gather.3.cloned.1.call-done = f32[8192,256]{0,1:T(8,128)} async-done(((f32[256,256]{0,1:T(8,128)}), f32[8192,256]{0,1:T(8,128)}) %all-gather.3.cloned.1.call-update) | async-done | bytes 8388624 | tf_op jit(solution)/shard_map/all_gather | solution.py:65
  232.4 6.8 %copy.42 = f32[32,8,32,256]{3,2,1,0:T(8,128)S(1)} copy(f32[32,8,32,256]{3,1,2,0:T(8,128)} %bitcast.86) | data formatting | bytes 16777216
  239.3 1.9 bitcast_reduce_fusion
  (127 shorter events, 40.6 us)
Async XLA Ops:
  7.2 19.4 %copy-start = (bf16[24,128,128]{2,1,0:T(8,128)(2,1)S(1)}, bf16[24,128,128]{2,1,0:T(8,128)(2,1)}, u32[]{:S(2)}) copy-start(bf16[24,128,128]{2,1,0:T(8,128)(2,1)} %param.17) | copy-start | bytes 2359300
  7.2 225.2 %all-gather.3.cloned.1.call-start = ((), (), s32[]{:S(2)}) async-start(), calls=%async_computation | async-start | bytes 8650752 | tf_op jit(solution)/shard_map/all_gather | solution.py:65
  9.2 14.0 %copy-start.5 = (s32[24]{0:T(128)S(1)}, s32[24]{0:T(128)}, u32[]{:S(2)}) copy-start(s32[24]{0:T(128)} %param.19) | copy-start | bytes 292
  9.2 14.1 %copy-start.6 = (s32[24]{0:T(128)S(1)}, s32[24]{0:T(128)}, u32[]{:S(2)}) copy-start(s32[24]{0:T(128)} %param.18) | copy-start | bytes 292
  10.1 14.8 %collective-permute-start.1 = (bf16[128,256]{1,0:T(8,128)(2,1)S(1)}, bf16[128,256]{1,0:T(8,128)(2,1)S(1)}, u32[]{:S(2)}, u32[]{:S(2)}) collective-permute-start(bf16[128,256]{1,0:T(8,128)(2,1)S(1)} %broadcast_select_fusion.14), channel_id=1, source_target_pairs={{0,31},{1,0},{2,1},{3,2},{4,3},{5,4},{6,5},{7,6},{8,7},{9,8},{10,9... | collective-permute-start | bytes 196616 | tf_op jit(solution)/shard_map/ppermute | solution.py:13
  17.5 7.4 %collective-permute-start = (bf16[128,256]{1,0:T(8,128)(2,1)S(1)}, bf16[128,256]{1,0:T(8,128)(2,1)S(1)}, u32[]{:S(2)}, u32[]{:S(2)}) collective-permute-start(bf16[128,256]{1,0:T(8,128)(2,1)S(1)} %broadcast_select_fusion.19), channel_id=1, source_target_pairs={{0,1},{1,2},{2,3},{3,4},{4,5},{5,6},{6,7},{7,8},{8,9},{9,10},{10,1... | collective-permute-start | bytes 196616 | tf_op jit(solution)/shard_map/ppermute | solution.py:13
  18.6 6.4 %collective-permute-start.2 = (bf16[128,256]{1,0:T(8,128)(2,1)S(1)}, bf16[128,256]{1,0:T(8,128)(2,1)S(1)}, u32[]{:S(2)}, u32[]{:S(2)}) collective-permute-start(bf16[128,256]{1,0:T(8,128)(2,1)S(1)} %broadcast_select_fusion.9), channel_id=1, source_target_pairs={{0,16},{1,17},{2,18},{3,19},{4,20},{5,21},{6,22},{7,23},{8,24},{9,... | collective-permute-start | bytes 196616 | tf_op jit(solution)/shard_map/ppermute | solution.py:13
  19.6 6.3 %collective-permute-start.3 = (bf16[128,256]{1,0:T(8,128)(2,1)S(1)}, bf16[128,256]{1,0:T(8,128)(2,1)S(1)}, u32[]{:S(2)}, u32[]{:S(2)}) collective-permute-start(bf16[128,256]{1,0:T(8,128)(2,1)S(1)} %broadcast_select_fusion.4), channel_id=1, source_target_pairs={{0,16},{1,17},{2,18},{3,19},{4,20},{5,21},{6,22},{7,23},{8,24},{9,... | collective-permute-start | bytes 196616 | tf_op jit(solution)/shard_map/ppermute | solution.py:13
  32.5 3.3 %copy-start.1 = (bf16[512,256]{1,0:T(8,128)(2,1)S(1)}, bf16[512,256]{1,0:T(8,128)(2,1)}, u32[]{:S(2)}) copy-start(bf16[512,256]{1,0:T(8,128)(2,1)} %param.15) | copy-start | bytes 786436
  32.5 3.3 %copy-start.2 = (bf16[512,256]{1,0:T(8,128)(2,1)S(1)}, bf16[512,256]{1,0:T(8,128)(2,1)}, u32[]{:S(2)}) copy-start(bf16[512,256]{1,0:T(8,128)(2,1)} %param.13) | copy-start | bytes 786436
  32.5 3.4 %copy-start.3 = (bf16[256,256]{1,0:T(8,128)(2,1)S(1)}, bf16[256,256]{1,0:T(8,128)(2,1)}, u32[]{:S(2)}) copy-start(bf16[256,256]{1,0:T(8,128)(2,1)} %param.16) | copy-start | bytes 393220
  39.8 8.5 %collective-permute-start.4 = (bf16[128,256]{1,0:T(8,128)(2,1)S(1)}, bf16[128,256]{1,0:T(8,128)(2,1)S(1)}, u32[]{:S(2)}, u32[]{:S(2)}) collective-permute-start(bf16[128,256]{1,0:T(8,128)(2,1)S(1)} %broadcast_select_fusion.18), channel_id=1, source_target_pairs={{0,1},{1,2},{2,3},{3,4},{4,5},{5,6},{6,7},{7,8},{8,9},{9,10},{10,1... | collective-permute-start | bytes 196616 | tf_op jit(solution)/shard_map/ppermute | solution.py:13
  39.9 8.3 %collective-permute-start.5 = (bf16[128,256]{1,0:T(8,128)(2,1)S(1)}, bf16[128,256]{1,0:T(8,128)(2,1)S(1)}, u32[]{:S(2)}, u32[]{:S(2)}) collective-permute-start(bf16[128,256]{1,0:T(8,128)(2,1)S(1)} %broadcast_select_fusion.13), channel_id=1, source_target_pairs={{0,31},{1,0},{2,1},{3,2},{4,3},{5,4},{6,5},{7,6},{8,7},{9,8},{10,9... | collective-permute-start | bytes 196616 | tf_op jit(solution)/shard_map/ppermute | solution.py:13
  45.3 5.7 %collective-permute-start.6 = (bf16[128,256]{1,0:T(8,128)(2,1)S(1)}, bf16[128,256]{1,0:T(8,128)(2,1)S(1)}, u32[]{:S(2)}, u32[]{:S(2)}) collective-permute-start(bf16[128,256]{1,0:T(8,128)(2,1)S(1)} %broadcast_select_fusion.8), channel_id=1, source_target_pairs={{0,16},{1,17},{2,18},{3,19},{4,20},{5,21},{6,22},{7,23},{8,24},{9,... | collective-permute-start | bytes 196616 | tf_op jit(solution)/shard_map/ppermute | solution.py:13
  45.4 6.4 %collective-permute-start.7 = (bf16[128,256]{1,0:T(8,128)(2,1)S(1)}, bf16[128,256]{1,0:T(8,128)(2,1)S(1)}, u32[]{:S(2)}, u32[]{:S(2)}) collective-permute-start(bf16[128,256]{1,0:T(8,128)(2,1)S(1)} %broadcast_select_fusion.3), channel_id=1, source_target_pairs={{0,16},{1,17},{2,18},{3,19},{4,20},{5,21},{6,22},{7,23},{8,24},{9,... | collective-permute-start | bytes 196616 | tf_op jit(solution)/shard_map/ppermute | solution.py:13
  68.1 8.6 %collective-permute-start.8 = (bf16[128,256]{1,0:T(8,128)(2,1)S(1)}, bf16[128,256]{1,0:T(8,128)(2,1)S(1)}, u32[]{:S(2)}, u32[]{:S(2)}) collective-permute-start(bf16[128,256]{1,0:T(8,128)(2,1)S(1)} %broadcast_select_fusion.17), channel_id=1, source_target_pairs={{0,1},{1,2},{2,3},{3,4},{4,5},{5,6},{6,7},{7,8},{8,9},{9,10},{10,1... | collective-permute-start | bytes 196616 | tf_op jit(solution)/shard_map/ppermute | solution.py:13
  68.3 8.5 %collective-permute-start.9 = (bf16[128,256]{1,0:T(8,128)(2,1)S(1)}, bf16[128,256]{1,0:T(8,128)(2,1)S(1)}, u32[]{:S(2)}, u32[]{:S(2)}) collective-permute-start(bf16[128,256]{1,0:T(8,128)(2,1)S(1)} %broadcast_select_fusion.12), channel_id=1, source_target_pairs={{0,31},{1,0},{2,1},{3,2},{4,3},{5,4},{6,5},{7,6},{8,7},{9,8},{10,9... | collective-permute-start | bytes 196616 | tf_op jit(solution)/shard_map/ppermute | solution.py:13
  73.9 5.2 %collective-permute-start.10 = (bf16[128,256]{1,0:T(8,128)(2,1)S(1)}, bf16[128,256]{1,0:T(8,128)(2,1)S(1)}, u32[]{:S(2)}, u32[]{:S(2)}) collective-permute-start(bf16[128,256]{1,0:T(8,128)(2,1)S(1)} %broadcast_select_fusion.7), channel_id=1, source_target_pairs={{0,16},{1,17},{2,18},{3,19},{4,20},{5,21},{6,22},{7,23},{8,24},{9,... | collective-permute-start | bytes 196616 | tf_op jit(solution)/shard_map/ppermute | solution.py:13
  73.9 5.9 %collective-permute-start.11 = (bf16[128,256]{1,0:T(8,128)(2,1)S(1)}, bf16[128,256]{1,0:T(8,128)(2,1)S(1)}, u32[]{:S(2)}, u32[]{:S(2)}) collective-permute-start(bf16[128,256]{1,0:T(8,128)(2,1)S(1)} %broadcast_select_fusion.2), channel_id=1, source_target_pairs={{0,16},{1,17},{2,18},{3,19},{4,20},{5,21},{6,22},{7,23},{8,24},{9,... | collective-permute-start | bytes 196616 | tf_op jit(solution)/shard_map/ppermute | solution.py:13
  96.1 8.5 %collective-permute-start.12 = (bf16[128,256]{1,0:T(8,128)(2,1)S(1)}, bf16[128,256]{1,0:T(8,128)(2,1)S(1)}, u32[]{:S(2)}, u32[]{:S(2)}) collective-permute-start(bf16[128,256]{1,0:T(8,128)(2,1)S(1)} %broadcast_select_fusion.16), channel_id=1, source_target_pairs={{0,1},{1,2},{2,3},{3,4},{4,5},{5,6},{6,7},{7,8},{8,9},{9,10},{10,1... | collective-permute-start | bytes 196616 | tf_op jit(solution)/shard_map/ppermute | solution.py:13
  96.2 8.3 %collective-permute-start.13 = (bf16[128,256]{1,0:T(8,128)(2,1)S(1)}, bf16[128,256]{1,0:T(8,128)(2,1)S(1)}, u32[]{:S(2)}, u32[]{:S(2)}) collective-permute-start(bf16[128,256]{1,0:T(8,128)(2,1)S(1)} %broadcast_select_fusion.11), channel_id=1, source_target_pairs={{0,31},{1,0},{2,1},{3,2},{4,3},{5,4},{6,5},{7,6},{8,7},{9,8},{10,9... | collective-permute-start | bytes 196616 | tf_op jit(solution)/shard_map/ppermute | solution.py:13
  101.6 5.2 %collective-permute-start.14 = (bf16[128,256]{1,0:T(8,128)(2,1)S(1)}, bf16[128,256]{1,0:T(8,128)(2,1)S(1)}, u32[]{:S(2)}, u32[]{:S(2)}) collective-permute-start(bf16[128,256]{1,0:T(8,128)(2,1)S(1)} %broadcast_select_fusion.6), channel_id=1, source_target_pairs={{0,16},{1,17},{2,18},{3,19},{4,20},{5,21},{6,22},{7,23},{8,24},{9,... | collective-permute-start | bytes 196616 | tf_op jit(solution)/shard_map/ppermute | solution.py:13
  102.1 5.4 %collective-permute-start.15 = (bf16[128,256]{1,0:T(8,128)(2,1)S(1)}, bf16[128,256]{1,0:T(8,128)(2,1)S(1)}, u32[]{:S(2)}, u32[]{:S(2)}) collective-permute-start(bf16[128,256]{1,0:T(8,128)(2,1)S(1)} %broadcast_select_fusion.1), channel_id=1, source_target_pairs={{0,16},{1,17},{2,18},{3,19},{4,20},{5,21},{6,22},{7,23},{8,24},{9,... | collective-permute-start | bytes 196616 | tf_op jit(solution)/shard_map/ppermute | solution.py:13
  124.6 8.7 %collective-permute-start.16 = (bf16[128,256]{1,0:T(8,128)(2,1)S(1)}, bf16[128,256]{1,0:T(8,128)(2,1)S(1)}, u32[]{:S(2)}, u32[]{:S(2)}) collective-permute-start(bf16[128,256]{1,0:T(8,128)(2,1)S(1)} %broadcast_select_fusion.15), channel_id=1, source_target_pairs={{0,1},{1,2},{2,3},{3,4},{4,5},{5,6},{6,7},{7,8},{8,9},{9,10},{10,1... | collective-permute-start | bytes 196616 | tf_op jit(solution)/shard_map/ppermute | solution.py:13
  124.8 8.5 %collective-permute-start.17 = (bf16[128,256]{1,0:T(8,128)(2,1)S(1)}, bf16[128,256]{1,0:T(8,128)(2,1)S(1)}, u32[]{:S(2)}, u32[]{:S(2)}) collective-permute-start(bf16[128,256]{1,0:T(8,128)(2,1)S(1)} %broadcast_select_fusion.10), channel_id=1, source_target_pairs={{0,31},{1,0},{2,1},{3,2},{4,3},{5,4},{6,5},{7,6},{8,7},{9,8},{10,9... | collective-permute-start | bytes 196616 | tf_op jit(solution)/shard_map/ppermute | solution.py:13
  130.4 5.2 %collective-permute-start.18 = (bf16[128,256]{1,0:T(8,128)(2,1)S(1)}, bf16[128,256]{1,0:T(8,128)(2,1)S(1)}, u32[]{:S(2)}, u32[]{:S(2)}) collective-permute-start(bf16[128,256]{1,0:T(8,128)(2,1)S(1)} %broadcast_select_fusion.5), channel_id=1, source_target_pairs={{0,16},{1,17},{2,18},{3,19},{4,20},{5,21},{6,22},{7,23},{8,24},{9,... | collective-permute-start | bytes 196616 | tf_op jit(solution)/shard_map/ppermute | solution.py:13
  130.8 5.4 %collective-permute-start.19 = (bf16[128,256]{1,0:T(8,128)(2,1)S(1)}, bf16[128,256]{1,0:T(8,128)(2,1)S(1)}, u32[]{:S(2)}, u32[]{:S(2)}) collective-permute-start(bf16[128,256]{1,0:T(8,128)(2,1)S(1)} %broadcast_select_fusion), channel_id=1, source_target_pairs={{0,16},{1,17},{2,18},{3,19},{4,20},{5,21},{6,22},{7,23},{8,24},{9,... | collective-permute-start | bytes 196616 | tf_op jit(solution)/shard_map/ppermute | solution.py:13
  145.4 3.5 %copy-start.4 = (bf16[512,256]{1,0:T(8,128)(2,1)S(1)}, bf16[512,256]{1,0:T(8,128)(2,1)}, u32[]{:S(2)}) copy-start(bf16[512,256]{1,0:T(8,128)(2,1)} %param.14) | copy-start | bytes 786436
Sparse Core Ops, SparseCore 0:
  150.4 82.0 all-gather.2
